TPU v7x, 512 devices: a whole 4x8x8 slice. The times are simulated.
512 devices in a mesh: expert: 8 (over x, core), tensor: 64 (over y, z).
Axes of the slice: x: 4, y: 8, z: 8, core: 2. Of those that a mesh axis runs over, the one named last changes fastest.
Arguments:
- tokens: bfloat16 [1536, 6144], P('tensor'), may hold values from -6 to 6
- expert_ids: int32 [1536, 2], P('tensor'), may hold values from 0 to 7, all different within a row; in each aligned block of 24 rows (0 to 23, 24 to 47, ...) at most 12 rows name the same one
- gate_units: int32 [1536, 2], P('tensor'), may hold values from 1 to 65535
- gate_weight: bfloat16 [8, 6144, 8192], P('expert', None, 'tensor'), may hold values from -0.078125 to 0.078125
- up_weight: bfloat16 [8, 6144, 8192], P('expert', None, 'tensor'), may hold values from -0.078125 to 0.078125
- down_weight: bfloat16 [8, 6144, 8192], P('expert', 'tensor'), may hold values from -0.0625 to 0.0625
Outputs:
- expert_mix: bfloat16 [1536, 6144], P('tensor', 'expert')
Inputs may be any that keep to these rules, and one draw needn't show every extreme that they name: `expert_ids`: within each aligned block of 24 rows (the tokens of one tensor index) the two ids of a row differ and no expert is named by more than 12 rows; in every draw some expert is named by exactly 12 rows of some block, and every expert is named somewhere.
All inputs are finite; a program needn't handle non-finite values.
Results may differ from a plain program's by a relative error of at most 0.0057.
Values may be sent and summed in bfloat16 or wider, within the bound.
A program may use at most 128 MiB of HBM per device.

v0:
```python
import jax
import jax.numpy as jnp
from jax import lax
from jax.sharding import PartitionSpec as P


def slot_tables(expert_ids, gate_units, expert_id, capacity):
    tok_rows = expert_ids.shape[0]
    top_count = expert_ids.shape[1]
    flat_route = expert_ids.reshape(-1)
    matches = (flat_route == expert_id).astype(jnp.int32)
    slot_rank = jnp.cumsum(matches) - matches
    slot_ids = jnp.arange(capacity, dtype=jnp.int32)
    assignment = jnp.where(
        (slot_rank[None, :] == slot_ids[:, None]) & (matches[None, :] == 1), 1.0, 0.0
    ).astype(jnp.float32)
    positions = jnp.arange(tok_rows * top_count, dtype=jnp.int32) // top_count
    owners = (positions[:, None] == jnp.arange(tok_rows, dtype=jnp.int32)[None, :]).astype(
        jnp.float32
    )
    unit_vals = gate_units.astype(jnp.float32)
    shares = unit_vals / jnp.sum(unit_vals, axis=1, keepdims=True)
    picker = jnp.dot(
        assignment, owners, precision=lax.Precision.HIGHEST, preferred_element_type=jnp.float32
    )
    weighted = jnp.dot(
        assignment,
        owners * shares.reshape(-1)[:, None],
        precision=lax.Precision.HIGHEST,
        preferred_element_type=jnp.float32,
    )
    return (picker, weighted)


def local(tokens, expert_ids, gate_units, gate_weight, up_weight, down_weight):
    experts = lax.axis_size("expert")
    expert_id = lax.axis_index("expert")
    tok_rows = tokens.shape[0]
    capacity = min(tok_rows, 4 * tok_rows // experts)
    picker, weighted = slot_tables(expert_ids, gate_units, expert_id, capacity)
    picked = jnp.dot(
        picker.astype(jnp.bfloat16), tokens, preferred_element_type=jnp.float32
    ).astype(jnp.bfloat16)
    w_gate = gate_weight[0]
    w_up = up_weight[0]
    w_down = down_weight[0]
    shard_piece = lax.all_gather(picked, "tensor", axis=0, tiled=True)
    gate_vals = jnp.dot(shard_piece, w_gate, preferred_element_type=jnp.float32)
    up_vals = jnp.dot(shard_piece, w_up, preferred_element_type=jnp.float32)
    hidden = (jax.nn.silu(gate_vals) * up_vals).astype(jnp.bfloat16)
    gathered = lax.all_gather(hidden, "tensor", axis=1, tiled=True)
    projected = lax.dot_general(
        gathered, w_down, (((1,), (1,)), ((), ())), preferred_element_type=jnp.float32
    )
    outputs = projected.astype(jnp.bfloat16)
    returned = lax.all_to_all(outputs, "tensor", split_axis=0, concat_axis=1, tiled=True)
    contribution = lax.dot_general(
        weighted,
        returned.astype(jnp.float32),
        (((0,), (0,)), ((), ())),
        precision=lax.Precision.HIGHEST,
        preferred_element_type=jnp.float32,
    )
    summed_all = lax.psum(contribution, "expert")
    col_width = contribution.shape[1] // experts
    mixed = lax.dynamic_slice_in_dim(summed_all, expert_id * col_width, col_width, 1)
    return mixed.astype(jnp.bfloat16)


def solution(mesh):
    return jax.shard_map(
        local,
        mesh=mesh,
        in_specs=(
            P("tensor", None),
            P("tensor", None),
            P("tensor", None),
            P("expert", None, "tensor"),
            P("expert", None, "tensor"),
            P("expert", "tensor", None),
        ),
        out_specs=P("tensor", "expert"),
        check_vma=False,
    )
```

profile of v0, /device:TPU:8, one launch (start us, length us, event | category | flops | bytes accessed | tf_op | source)
XLA Modules:
  0.0 349.5 jit_solution(7697855502720402069)
XLA Ops:
  6.5 0.0 copy-start
  6.5 0.0 all-gather.6.cloned.1.call-start
  6.5 0.8 compare_convert_fusion
  7.3 0.1 copy.17
  7.4 0.1 reshape.76
  7.5 0.1 reshape.79
  7.6 0.1 reduce-window.8
  7.7 0.1 reduce
  7.8 0.2 convolution_convert_fusion.1
  8.0 1.8 fusion
  9.9 0.0 all-gather.6.cloned.1.call-update
  9.9 0.0 all-gather.4.cloned.1.call-start
  9.9 124.4 %all-gather.6.cloned.1.call-done = bf16[64,12,6144]{2,1,0:T(8,128)(2,1)} async-done(((bf16[1,12,6144]{2,1,0:T(8,128)(2,1)}), bf16[64,12,6144]{2,1,0:T(8,128)(2,1)}) %all-gather.6.cloned.1.call-update) | async-done | bytes 9437200 | tf_op jit(solution)/shard_map/all_gather | solution.py:47
  134.3 13.7 %reshape.78 = bf16[768,6144]{1,0:T(8,128)(2,1)} reshape(bf16[64,12,6144]{2,1,0:T(8,128)(2,1)} %all-gather.6.cloned.1.call-done) | data formatting | bytes 18874368
  148.1 0.0 copy-done
  148.1 0.0 copy-start.1
  148.1 0.0 copy-start.4
  148.1 6.1 %fusion.5 = f32[768,128]{1,0:T(8,128)S(1)} fusion(bf16[768,6144]{1,0:T(8,128)(2,1)} %reshape.78, bf16[1,6144,128]{2,1,0:T(8,128)(2,1)S(1)} %copy-done), kind=kOutput, calls=%fused_computation.6 | convolution fusion | flops 1207959552 | bytes 11403264 | tf_op jit(solution)/shard_map/dot_general | solution.py:48
  154.2 0.3 copy-done.1
  154.5 0.4 copy-done.4
  154.9 0.0 copy-start.3
  154.9 0.0 copy-start.2
  155.0 3.3 fusion.10
  158.2 0.0 all-gather.4.cloned.1.call-update
  158.2 0.0 copy-done.3
  158.3 124.2 %all-gather.4.cloned.1.call-done = bf16[768,8192]{1,0:T(8,128)(2,1)} async-done(((bf16[768,128]{1,0:T(8,128)(2,1)}), bf16[768,8192]{1,0:T(8,128)(2,1)}) %all-gather.4.cloned.1.call-update) | async-done | bytes 12582928 | tf_op jit(solution)/shard_map/all_gather | solution.py:51
  282.5 0.0 copy-done.2
  282.5 8.6 %fusion.13 = bf16[768,96]{0,1:T(8,128)(2,1)S(1)} fusion(bf16[768,8192]{1,0:T(8,128)(2,1)} %all-gather.4.cloned.1.call-done, bf16[1,96,8192]{2,1,0:T(8,128)(2,1)S(1)} %copy-done.2), kind=kOutput, calls=%fused_computation.10 | convolution fusion | flops 1208033280 | bytes 14303232 | tf_op jit(solution)/shard_map/dot_general | solution.py:52
  291.1 0.2 copy.21
  291.3 0.8 all_to_all.14
  292.0 7.8 %all-to-all-start = ((bf16[64,12,96]{2,1,0:T(8,128)(2,1)}), bf16[64,12,96]{2,1,0:T(8,128)(2,1)S(1)}, u32[]{:S(2)}, u32[]{:S(2)}) async-start(bf16[64,12,96]{2,1,0:T(8,128)(2,1)} %all_to_all.14), calls=%async_computation | async-start | bytes 524288 | tf_op jit(solution)/shard_map/all_to_all | solution.py:56
  299.8 0.1 copy.20
  299.9 0.1 mul.20
  300.0 0.2 fusion.16
  300.2 12.0 %all-to-all-done = bf16[64,12,96]{2,1,0:T(8,128)(2,1)S(1)} async-done(((bf16[64,12,96]{2,1,0:T(8,128)(2,1)}), bf16[64,12,96]{2,1,0:T(8,128)(2,1)S(1)}, u32[]{:S(2)}, u32[]{:S(2)}) %all-to-all-start) | async-done | bytes 147488 | tf_op jit(solution)/shard_map/all_to_all | solution.py:56
  312.2 0.1 copy.22
  312.2 0.3 all_to_all.17
  312.5 0.4 fusion.39
  313.0 29.1 %all-reduce.1 = bf16[24,6144]{1,0:T(8,128)(2,1)S(1)} all-reduce(f32[24,6144]{1,0:T(8,128)S(1)} %fusion.39), channel_id=1, replica_groups=mesh['expert'=8,'tensor'=64] {'expert'}, use_global_device_ids=true, to_apply=%region_2.3 | all-reduce | flops 147456 | bytes 884736 | tf_op jit(solution)/shard_map/psum | solution.py:64
  342.0 0.6 dynamic-slice_convert_fusion
  (5 shorter events, 0.0 us)
Async XLA Ops:
  6.5 141.6 %copy-start = (bf16[1,6144,128]{2,1,0:T(8,128)(2,1)S(1)}, bf16[1,6144,128]{2,1,0:T(8,128)(2,1)}, u32[]{:S(2)}) copy-start(bf16[1,6144,128]{2,1,0:T(8,128)(2,1)} %param.9) | copy-start | bytes 4718596
  6.5 127.8 %all-gather.6.cloned.1.call-start = ((), (), s32[]{:S(2)}) async-start(), calls=%async_computation.2 | async-start | bytes 12779520 | tf_op jit(solution)/shard_map/all_gather | solution.py:47
  9.9 272.6 %all-gather.4.cloned.1.call-start = ((), (), s32[]{:S(2)}) async-start(), calls=%async_computation.1 | async-start | bytes 12779520 | tf_op jit(solution)/shard_map/all_gather | solution.py:51
  148.1 6.4 %copy-start.1 = (bf16[768,6144]{1,0:T(8,128)(2,1)S(1)}, bf16[768,6144]{1,0:T(8,128)(2,1)}, u32[]{:S(2)}) copy-start(bf16[768,6144]{1,0:T(8,128)(2,1)} %reshape.78) | copy-start | bytes 28311556
  148.1 6.9 %copy-start.4 = (bf16[1,6144,128]{2,1,0:T(8,128)(2,1)S(1)}, bf16[1,6144,128]{2,1,0:T(8,128)(2,1)}, u32[]{:S(2)}) copy-start(bf16[1,6144,128]{2,1,0:T(8,128)(2,1)} %param.10) | copy-start | bytes 4718596
  154.9 3.3 copy-start.3
  154.9 127.6 %copy-start.2 = (bf16[1,96,8192]{2,1,0:T(8,128)(2,1)S(1)}, bf16[1,96,8192]{2,1,0:T(8,128)(2,1)}, u32[]{:S(2)}) copy-start(bf16[1,96,8192]{2,1,0:T(8,128)(2,1)} %param.11) | copy-start | bytes 4718596
  292.0 20.1 %all-to-all-start = ((bf16[64,12,96]{2,1,0:T(8,128)(2,1)}), bf16[64,12,96]{2,1,0:T(8,128)(2,1)S(1)}, u32[]{:S(2)}, u32[]{:S(2)}) async-start(bf16[64,12,96]{2,1,0:T(8,128)(2,1)} %all_to_all.14), calls=%async_computation | async-start | bytes 524288 | tf_op jit(solution)/shard_map/all_to_all | solution.py:56
Sparse Core Ops, SparseCore 0:
  10.4 123.9 all-gather.5
  158.4 124.1 all-gather.3
where the time goes:
time: 350 us
  waiting for transfers between devices  261 us (75%)
  blocking collectives  29.1 us (8%)
  matrix products  20.7 us (6%)
  local copies, waits for them, and re-layouts  16.8 us (5%)
  between operations  13.5 us (4%)
  starting transfers between devices  7.81 us (2%)
    all_gather x1, waiting for transfers between devices, local(): shard_piece = lax.all_gather(picked, 'tensor', axis=0, tiled=True)  124 us
    all_gather x1, waiting for transfers between devices, local(): gathered = lax.all_gather(hidden, 'tensor', axis=1, tiled=True)  124 us
    psum x1, blocking collectives, local(): summed_all = lax.psum(contribution, 'expert')  29.1 us
    unnamed x11, local copies, waits for them, and re-layouts  14.5 us
    all_to_all x1, waiting for transfers between devices, local(): lax.all_to_all(outputs, 'tensor', split_axis=0, concat_axis=1, tiled=True)  12 us
    dot_general x1, matrix products, local(): lax.dot_general(gathered, w_down, (((1,), (1,)), ((), ())), preferred_ele...  8.57 us
    all_to_all x1, starting transfers between devices, local(): lax.all_to_all(outputs, 'tensor', split_axis=0, concat_axis=1, tiled=True)  7.77 us
  transfers between devices with their start and end apart: 3, of which 3 were waited for; matrix products, arithmetic and copies ran while one was open for 0% of the time, Pallas kernels for 0%

commit v1 on v0

--- a/solution.py
+++ b/solution.py
@@ -2,6 +2,11 @@
 import jax.numpy as jnp
 from jax import lax
 from jax.sharding import PartitionSpec as P
+
+
+def swapped_in(x, axis, dim):
+    sent = jnp.stack([x] * lax.axis_size(axis))
+    return jnp.concatenate(lax.all_to_all(sent, axis, 0, 0), axis=dim)
 
 
 def slot_tables(expert_ids, gate_units, expert_id, capacity):
@@ -44,7 +49,7 @@
     w_gate = gate_weight[0]
     w_up = up_weight[0]
     w_down = down_weight[0]
-    shard_piece = lax.all_gather(picked, "tensor", axis=0, tiled=True)
+    shard_piece = swapped_in(picked, "tensor", 0)
     gate_vals = jnp.dot(shard_piece, w_gate, preferred_element_type=jnp.float32)
     up_vals = jnp.dot(shard_piece, w_up, preferred_element_type=jnp.float32)
     hidden = (jax.nn.silu(gate_vals) * up_vals).astype(jnp.bfloat16)

time: 350 us -> 591 us (1.69)
  blocking collectives: 29.1 us -> 351 us
  waiting for transfers between devices: 261 us -> 174 us
  local copies, waits for them, and re-layouts: 16.8 us -> 22.8 us
    all_to_all x0 -> x1, blocking collectives: none -> 322 us  [swapped_in(): return jnp.concatenate(lax.all_to_all(sent, axis, 0, 0), axis=dim)]
    all_gather x1 -> x0, waiting for transfers between devices: 124 us -> none  [local(): shard_piece = lax.all_gather(picked, 'tensor', axis=0, tiled=True)]
    all_gather x1, waiting for transfers between devices: 124 us -> 162 us  [local(): gathered = lax.all_gather(hidden, 'tensor', axis=1, tiled=True)]
    unnamed x11 -> x10, local copies, waits for them, and re-layouts: 14.5 us -> 0.71 us
    reshape x0 -> x1, local copies, waits for them, and re-layouts: none -> 13.7 us  [swapped_in(): return jnp.concatenate(lax.all_to_all(sent, axis, 0, 0), axis=dim)]
    another operation x0 -> x1, local copies, waits for them, and re-layouts: none -> 6.04 us  [swapped_in(): sent = jnp.stack([x] * lax.axis_size(axis))]
  transfers between devices with their start and end apart: 3 -> 2, of which waited for: 3 -> 2; matrix products, arithmetic and copies ran while one was open for 0% -> 0% of each run, Pallas kernels for 0% -> 0%
where the time goes in v1:
time: 591 us; the launch traced here: 590 us
  blocking collectives  351 us (59%)
  waiting for transfers between devices  174 us (29%)
  local copies, waits for them, and re-layouts  22.8 us (4%)
  matrix products  20 us (3%)
  between operations  13.5 us (2%)
  starting transfers between devices  7.77 us (1%)
    all_to_all x1, blocking collectives, swapped_in(): return jnp.concatenate(lax.all_to_all(sent, axis, 0, 0), axis=dim)  322 us
    all_gather x1, waiting for transfers between devices, local(): gathered = lax.all_gather(hidden, 'tensor', axis=1, tiled=True)  162 us
    psum x1, blocking collectives, local(): summed_all = lax.psum(contribution, 'expert')  29.1 us
    reshape x1, local copies, waits for them, and re-layouts, swapped_in(): return jnp.concatenate(lax.all_to_all(sent, axis, 0, 0), axis=dim)  13.7 us
    all_to_all x1, waiting for transfers between devices, local(): lax.all_to_all(outputs, 'tensor', split_axis=0, concat_axis=1, tiled=True)  12 us
  transfers between devices with their start and end apart: 2, of which 2 were waited for; matrix products, arithmetic and copies ran while one was open for 0% of the time, Pallas kernels for 0%

profile of v1, /device:TPU:8, one launch (start us, length us, event | category | flops | bytes accessed | tf_op | source)
XLA Modules:
  0.0 589.9 jit_solution(12311861562303446101)
XLA Ops:
  6.5 0.0 copy-start
  6.5 0.0 all-gather.2.cloned.1.call-start
  6.5 0.8 compare_convert_fusion
  7.3 0.1 copy.11
  7.4 0.1 reshape.82
  7.5 0.1 reshape.83
  7.6 0.1 reduce-window.8
  7.7 0.1 reduce
  7.8 0.2 convolution_convert_fusion.1
  8.0 1.2 convolution_convert_fusion
  9.2 6.0 %stack.2 = bf16[64,12,6144]{2,1,0:T(8,128)(2,1)} broadcast(bf16[12,6144]{1,0:T(8,128)(2,1)S(1)} %convolution_convert_fusion), dimensions={1,2} | broadcast | bytes 9584640 | tf_op jit(solution)/shard_map/stack | solution.py:8
  15.2 321.8 %all_to_all.24 = bf16[64,12,6144]{2,1,0:T(8,128)(2,1)} all-to-all(bf16[64,12,6144]{2,1,0:T(8,128)(2,1)} %stack.2), channel_id=1, replica_groups=mesh['expert'=8,'tensor'=64] {'tensor'}, dimensions={0} | all-to-all | bytes 18874368 | tf_op jit(solution)/shard_map/all_to_all | solution.py:9
  337.0 13.7 %reshape.80 = bf16[768,6144]{1,0:T(8,128)(2,1)} reshape(bf16[64,12,6144]{2,1,0:T(8,128)(2,1)} %all_to_all.24) | data formatting | bytes 18874368 | tf_op jit(solution)/shard_map/reshape | solution.py:9
  350.7 0.0 copy-done
  350.8 0.0 copy-start.1
  350.8 0.0 copy-start.4
  350.8 6.1 %fusion.4 = f32[768,128]{1,0:T(8,128)S(1)} fusion(bf16[768,6144]{1,0:T(8,128)(2,1)} %reshape.80, bf16[1,6144,128]{2,1,0:T(8,128)(2,1)S(1)} %copy-done), kind=kOutput, calls=%fused_computation.5 | convolution fusion | flops 1207959552 | bytes 11403264 | tf_op jit(solution)/shard_map/dot_general | solution.py:53
  356.9 0.3 copy-done.1
  357.2 0.4 copy-done.4
  357.6 0.0 copy-start.3
  357.6 0.0 copy-start.2
  357.6 3.3 fusion.9
  360.9 0.0 all-gather.2.cloned.1.call-update
  360.9 0.0 copy-done.3
  360.9 162.0 %all-gather.2.cloned.1.call-done = bf16[768,8192]{1,0:T(8,128)(2,1)} async-done(((bf16[768,128]{1,0:T(8,128)(2,1)}), bf16[768,8192]{1,0:T(8,128)(2,1)}) %all-gather.2.cloned.1.call-update) | async-done | bytes 12582928 | tf_op jit(solution)/shard_map/all_gather | solution.py:56
  522.9 0.0 copy-done.2
  522.9 8.6 %fusion.12 = bf16[768,96]{0,1:T(8,128)(2,1)S(1)} fusion(bf16[768,8192]{1,0:T(8,128)(2,1)} %all-gather.2.cloned.1.call-done, bf16[1,96,8192]{2,1,0:T(8,128)(2,1)S(1)} %copy-done.2), kind=kOutput, calls=%fused_computation.9 | convolution fusion | flops 1208033280 | bytes 14303232 | tf_op jit(solution)/shard_map/dot_general | solution.py:57
  531.5 0.2 copy.15
  531.7 0.8 all_to_all.18
  532.4 7.8 %all-to-all-start.1 = ((bf16[64,12,96]{2,1,0:T(8,128)(2,1)}), bf16[64,12,96]{2,1,0:T(8,128)(2,1)S(1)}, u32[]{:S(2)}, u32[]{:S(2)}) async-start(bf16[64,12,96]{2,1,0:T(8,128)(2,1)} %all_to_all.18), calls=%async_computation.1 | async-start | bytes 524288 | tf_op jit(solution)/shard_map/all_to_all | solution.py:61
  540.2 0.1 copy.14
  540.3 0.1 mul.20
  540.4 0.2 fusion.15
  540.6 12.0 %all-to-all-done.1 = bf16[64,12,96]{2,1,0:T(8,128)(2,1)S(1)} async-done(((bf16[64,12,96]{2,1,0:T(8,128)(2,1)}), bf16[64,12,96]{2,1,0:T(8,128)(2,1)S(1)}, u32[]{:S(2)}, u32[]{:S(2)}) %all-to-all-start.1) | async-done | bytes 147488 | tf_op jit(solution)/shard_map/all_to_all | solution.py:61
  552.6 0.1 copy.16
  552.6 0.3 all_to_all.21
  552.9 0.4 fusion.38
  553.4 29.1 %all-reduce.1 = bf16[24,6144]{1,0:T(8,128)(2,1)S(1)} all-reduce(f32[24,6144]{1,0:T(8,128)S(1)} %fusion.38), channel_id=1, replica_groups=mesh['expert'=8,'tensor'=64] {'expert'}, use_global_device_ids=true, to_apply=%region_2.3 | all-reduce | flops 147456 | bytes 884736 | tf_op jit(solution)/shard_map/psum | solution.py:69
  582.5 0.6 dynamic-slice_convert_fusion
  (5 shorter events, 0.0 us)
Async XLA Ops:
  6.5 344.2 %copy-start = (bf16[1,6144,128]{2,1,0:T(8,128)(2,1)S(1)}, bf16[1,6144,128]{2,1,0:T(8,128)(2,1)}, u32[]{:S(2)}) copy-start(bf16[1,6144,128]{2,1,0:T(8,128)(2,1)} %param.9) | copy-start | bytes 4718596
  6.5 516.4 %all-gather.2.cloned.1.call-start = ((), (), s32[]{:S(2)}) async-start(), calls=%async_computation.2 | async-start | bytes 12779520 | tf_op jit(solution)/shard_map/all_gather | solution.py:56
  350.8 6.4 %copy-start.1 = (bf16[768,6144]{1,0:T(8,128)(2,1)S(1)}, bf16[768,6144]{1,0:T(8,128)(2,1)}, u32[]{:S(2)}) copy-start(bf16[768,6144]{1,0:T(8,128)(2,1)} %reshape.80) | copy-start | bytes 28311556
  350.8 6.9 %copy-start.4 = (bf16[1,6144,128]{2,1,0:T(8,128)(2,1)S(1)}, bf16[1,6144,128]{2,1,0:T(8,128)(2,1)}, u32[]{:S(2)}) copy-start(bf16[1,6144,128]{2,1,0:T(8,128)(2,1)} %param.10) | copy-start | bytes 4718596
  357.6 3.3 copy-start.3
  357.6 165.3 %copy-start.2 = (bf16[1,96,8192]{2,1,0:T(8,128)(2,1)S(1)}, bf16[1,96,8192]{2,1,0:T(8,128)(2,1)}, u32[]{:S(2)}) copy-start(bf16[1,96,8192]{2,1,0:T(8,128)(2,1)} %param.11) | copy-start | bytes 4718596
  532.4 20.1 %all-to-all-start.1 = ((bf16[64,12,96]{2,1,0:T(8,128)(2,1)}), bf16[64,12,96]{2,1,0:T(8,128)(2,1)S(1)}, u32[]{:S(2)}, u32[]{:S(2)}) async-start(bf16[64,12,96]{2,1,0:T(8,128)(2,1)} %all_to_all.18), calls=%async_computation.1 | async-start | bytes 524288 | tf_op jit(solution)/shard_map/all_to_all | solution.py:61
Sparse Core Ops, SparseCore 0:
  361.0 161.8 all-gather.1
